TPU v7x, 128 devices: a whole 4x4x4 slice. The times are simulated.
128 devices in a mesh: row: 16 (over z, x), col: 8 (over y, core).
Axes of the slice: x: 4, y: 4, z: 4, core: 2. Of those that a mesh axis runs over, the one named last changes fastest.
Arguments:
- tokens: bfloat16 [2048, 4096], P('row', 'col'), may hold values from -6 to 6
- up_weight: bfloat16 [128, 8, 128, 128], P(('col', 'row')), may hold values from -0.1875 to 0.1875
- up_rows: int32 [128, 8], P('col'), may hold values from 0 to 31, as said below
- down_weight: bfloat16 [128, 8, 128, 128], P(('col', 'row')), may hold values from -0.09375 to 0.09375
- down_cols: int32 [128, 8], P('col'), may hold values from 0 to 31, as said below
- grad_out: bfloat16 [2048, 4096], P('row', 'col'), may hold values from -6 to 6
Outputs:
- layer_out: bfloat16 [2048, 4096], P('row', 'col')
- grad_tokens: bfloat16 [2048, 4096], P('row', 'col')
- grad_up: bfloat16 [128, 8, 128, 128], P(('col', 'row'))
- grad_down: bfloat16 [128, 8, 128, 128], P(('col', 'row'))
Inputs may be any that keep to these rules, and one draw needn't show every extreme that they name: `up_rows`: row j lists 8 distinct block rows of the up projection's block column j in rising order; they are that block column's only nonzero blocks. `down_cols`: row i lists 8 distinct block columns of the down projection's block row i in rising order; they are that block row's only nonzero blocks.
All inputs are finite; a program needn't handle non-finite values.
Results may differ from a plain program's by a relative error of at most 0.019.
Values may be sent and summed in bfloat16 or wider, within the bound.
No kernel may reach another device: no remote copies, remote signals or barrier semaphores. Data moves between devices by JAX's collectives and lax.ppermute only.
A program may use at most 128 MiB of HBM per device.

v0:
```python
import math
import jax
import jax.numpy as jnp
from jax import lax
from jax.sharding import PartitionSpec as P


def gelu_tanh(values):
    return jax.nn.gelu(values, approximate=True)


def up_apply(token_blocks, panel_blocks, row_ids):
    summed = jnp.zeros(
        (token_blocks.shape[0], panel_blocks.shape[0], panel_blocks.shape[3]), jnp.float32
    )
    for slot_index in range(panel_blocks.shape[1]):
        picked = jnp.take(token_blocks, row_ids[:, slot_index], axis=1)
        summed = summed + jnp.einsum(
            "tja,jab->tjb", picked, panel_blocks[:, slot_index], preferred_element_type=jnp.float32
        )
    return summed


def up_transpose(grad_piece, panel_blocks, row_ids, block_count):
    summed = jnp.zeros((grad_piece.shape[0], block_count, panel_blocks.shape[2]), jnp.float32)
    for slot_index in range(panel_blocks.shape[1]):
        product = jnp.einsum(
            "tjb,jab->tja",
            grad_piece,
            panel_blocks[:, slot_index],
            preferred_element_type=jnp.float32,
        )
        summed = summed.at[:, row_ids[:, slot_index], :].add(product)
    return summed


def down_apply(hidden_piece, grad_blocks, panel_blocks, col_ids, block_count):
    tok_rows = hidden_piece.shape[0]
    out_part = jnp.zeros((tok_rows, block_count, panel_blocks.shape[3]), jnp.float32)
    grad_piece = jnp.zeros((tok_rows, panel_blocks.shape[0], panel_blocks.shape[2]), jnp.float32)
    for slot_index in range(panel_blocks.shape[1]):
        weight_slot = panel_blocks[:, slot_index]
        product = jnp.einsum(
            "tia,iab->tib", hidden_piece, weight_slot, preferred_element_type=jnp.float32
        )
        out_part = out_part.at[:, col_ids[:, slot_index], :].add(product)
        picked = jnp.take(grad_blocks, col_ids[:, slot_index], axis=1)
        grad_piece = grad_piece + jnp.einsum(
            "tib,iab->tia", picked, weight_slot, preferred_element_type=jnp.float32
        )
    return (out_part, grad_piece)


def per_device(tokens, up_weight, up_rows, down_weight, down_cols, grad_out):
    tok_rows = tokens.shape[0]
    block_size = up_weight.shape[2]
    slot_count = up_weight.shape[1]
    token_whole, grad_whole = (
        lax.all_gather(tokens, "col", axis=1, tiled=True),
        lax.all_gather(grad_out, "col", axis=1, tiled=True),
    )
    block_count = token_whole.shape[1] // block_size
    token_blocks = token_whole.reshape(tok_rows, block_count, block_size)
    grad_blocks = grad_whole.reshape(tok_rows, block_count, block_size)
    row_ids = up_rows
    pre_act = up_apply(token_blocks, lax.all_gather(up_weight, "row", axis=0, tiled=True), row_ids)
    hidden = gelu_tanh(pre_act).astype(jnp.bfloat16)
    hidden_piece = hidden
    col_ids = down_cols
    added, grad_piece = down_apply(
        hidden_piece,
        grad_blocks,
        lax.all_gather(down_weight, "row", axis=0, tiled=True),
        col_ids,
        block_count,
    )
    grad_hidden = grad_piece
    out_sum = lax.psum_scatter(
        added.astype(jnp.bfloat16), "col", scatter_dimension=1, tiled=True
    ).astype(jnp.float32)
    layer_out = out_sum.reshape(tok_rows, -1).astype(jnp.bfloat16)
    pull_back = jax.vjp(gelu_tanh, pre_act)[1]
    grad_pre = pull_back(grad_hidden)[0].astype(jnp.bfloat16)
    row_ids = up_rows
    grad_piece = grad_pre
    input_part = up_transpose(
        grad_piece, lax.all_gather(up_weight, "row", axis=0, tiled=True), row_ids, block_count
    )
    input_sum = lax.psum_scatter(
        input_part.astype(jnp.bfloat16), "col", scatter_dimension=1, tiled=True
    ).astype(jnp.float32)
    grad_tokens = input_sum.reshape(tok_rows, -1).astype(jnp.bfloat16)
    hidden_piece = hidden
    col_ids = down_cols
    terms_list = []
    for down_slot_index in range(slot_count):
        down_picked = jnp.take(grad_blocks, col_ids[:, down_slot_index], axis=1)
        terms_list.append(
            jnp.einsum(
                "tia,tib->iab", hidden_piece, down_picked, preferred_element_type=jnp.float32
            )
        )
    down_sum = lax.psum_scatter(
        jnp.stack(terms_list, axis=1).astype(jnp.bfloat16), "row", scatter_dimension=0, tiled=True
    ).astype(jnp.float32)
    grad_piece = grad_pre
    row_ids = up_rows
    terms_list = []
    for slot_index in range(slot_count):
        picked = jnp.take(token_blocks, row_ids[:, slot_index], axis=1)
        terms_list.append(
            jnp.einsum("tja,tjb->jab", picked, grad_piece, preferred_element_type=jnp.float32)
        )
    up_sum = lax.psum_scatter(
        jnp.stack(terms_list, axis=1).astype(jnp.bfloat16), "row", scatter_dimension=0, tiled=True
    ).astype(jnp.float32)
    grad_scale = 1.0 / math.sqrt(tok_rows * lax.axis_size("row"))
    grad_up = (up_sum * grad_scale).astype(jnp.bfloat16)
    grad_down = (down_sum * grad_scale).astype(jnp.bfloat16)
    return (layer_out, grad_tokens, grad_up, grad_down)


def solution(mesh):
    return jax.shard_map(
        per_device,
        mesh=mesh,
        in_specs=(
            P("row", "col"),
            P(("col", "row"), None, None, None),
            P("col", None),
            P(("col", "row"), None, None, None),
            P("col", None),
            P("row", "col"),
        ),
        out_specs=(
            P("row", "col"),
            P("row", "col"),
            P(("col", "row"), None, None, None),
            P(("col", "row"), None, None, None),
        ),
        check_vma=False,
    )
```

profile of v0, /device:TPU:1, one launch (start us, length us, event | category | flops | bytes accessed | tf_op | source)
XLA Modules:
  0.0 460.6 jit_solution(11785073834474695060)
XLA Ops:
  7.2 1.7 copy.96
  8.9 1.7 copy.108
  16.1 21.2 %all-gather.5.cloned.1.call-done = bf16[128,4096]{0,1:T(8,128)(2,1)} async-done(((bf16[128,512]{0,1:T(8,128)(2,1)}), bf16[128,4096]{0,1:T(8,128)(2,1)}) %all-gather.5.cloned.1.call-update) | async-done | bytes 1048592 | tf_op jit(solution)/shard_map/all_gather | solution.py:59
  37.3 1.6 copy.97
  39.6 1.5 gather_fusion.1
  41.1 1.4 gather_fusion.2
  43.9 1.4 gather_fusion.4
  46.7 1.4 gather_fusion.7
  48.1 14.8 %all-gather.11.cloned.1.call-done = bf16[128,4096]{0,1:T(8,128)(2,1)} async-done(((bf16[128,512]{0,1:T(8,128)(2,1)}), bf16[128,4096]{0,1:T(8,128)(2,1)}) %all-gather.11.cloned.1.call-update) | async-done | bytes 1048592 | tf_op jit(solution)/shard_map/all_gather | solution.py:60
  62.9 1.6 copy.109
  66.6 1.4 gather_fusion.10
  68.0 1.4 gather_fusion.11
  69.4 1.4 gather_fusion.12
  70.8 1.4 gather_fusion.13
  72.2 1.4 gather_fusion.14
  73.6 1.4 gather_fusion.15
  75.1 41.1 %all-gather.7.cloned.1.call-done = bf16[16,8,128,128]{3,2,0,1:T(8,128)(2,1)} async-done(((bf16[1,8,128,128]{3,2,0,1:T(8,128)(2,1)}), bf16[16,8,128,128]{3,2,0,1:T(8,128)(2,1)}) %all-gather.7.cloned.1.call-update) | async-done | bytes 4194320 | tf_op jit(solution)/shard_map/all_gather | solution.py:66
  116.2 1.5 fusion.73
  117.8 1.6 convolution_add_fusion.13
  121.3 1.6 multiply_convert_fusion
  122.9 46.6 %all-gather.9.cloned.1.call-done = bf16[16,8,128,128]{3,2,0,1:T(8,128)(2,1)} async-done(((bf16[1,8,128,128]{3,2,0,1:T(8,128)(2,1)}), bf16[16,8,128,128]{3,2,0,1:T(8,128)(2,1)}) %all-gather.9.cloned.1.call-update) | async-done | bytes 4194320 | tf_op jit(solution)/shard_map/all_gather | solution.py:73
  169.5 2.3 fusion.83
  172.0 2.6 scatter_fusion
  174.6 2.3 fusion.84
  176.9 2.6 scatter_fusion.1
  179.5 2.3 fusion.85
  181.8 2.6 scatter_fusion.2
  184.5 2.3 fusion.86
  186.8 2.6 scatter_fusion.3
  189.4 2.3 fusion.87
  191.7 2.6 scatter_fusion.4
  194.3 2.3 fusion.88
  196.6 2.6 scatter_fusion.5
  199.2 2.3 fusion.89
  201.5 2.8 scatter_fusion.6
  204.3 2.3 fusion.90
  206.6 2.6 scatter_fusion.7
  210.4 1.7 fusion.56
  212.1 1.8 convolution_add_fusion.6
  217.7 2.5 fusion.75
  220.4 2.6 scatter_fusion.8
  223.0 2.5 fusion.76
  225.5 2.6 scatter_fusion.9
  228.1 2.5 fusion.77
  230.6 2.6 scatter_fusion.10
  233.2 2.5 fusion.78
  235.7 2.6 scatter_fusion.11
  238.3 2.5 fusion.79
  240.8 2.6 scatter_fusion.12
  243.4 2.5 fusion.80
  245.9 2.6 scatter_fusion.13
  248.6 2.5 fusion.81
  251.0 2.6 scatter_fusion.14
  253.6 2.5 fusion.82
  256.1 2.8 scatter_fusion.15
  260.1 2.4 fusion.3
  262.5 2.3 fusion.19
  264.8 2.3 fusion.5
  273.4 2.4 fusion.17
  275.8 2.3 fusion.21
  288.2 13.9 %reduce-scatter.11.cloned.1.call-done = bf16[128,4,128]{2,0,1:T(8,128)(2,1)} async-done(((bf16[128,32,128]{2,0,1:T(8,128)(2,1)}), bf16[128,4,128]{2,0,1:T(8,128)(2,1)}) %reduce-scatter.11.cloned.1.call-update) | async-done | bytes 131088 | tf_op jit(solution)/shard_map/reduce_scatter | solution.py:89
  303.9 145.3 %all-reduce.5.cloned.1.call-done = (bf16[16,8,128,128]{3,2,0,1:T(8,128)(2,1)}, bf16[16,8,128,128]{3,2,0,1:T(8,128)(2,1)}) async-done(((bf16[16,8,128,128]{3,2,0,1:T(8,128)(2,1)}, bf16[16,8,128,128]{3,2,0,1:T(8,128)(2,1)}), (bf16[16,8,128,128]{3,2,0,1:T(8,128)(2,1)}, bf16[16,8,128,128]{3,2,0,1:T(8,128)(2,1)})) %all-reduce.5.cloned.1.call-update) | async-done | bytes 8388624
  449.2 2.3 fusion.91
  451.5 2.3 fusion.92
  (122 shorter events, 37.3 us)
Async XLA Ops:
  7.2 30.2 %all-gather.5.cloned.1.call-start = ((), (), s32[]{:S(2)}) async-start(), calls=%async_computation.2 | async-start | bytes 1179648 | tf_op jit(solution)/shard_map/all_gather | solution.py:59
  8.9 54.0 %all-gather.11.cloned.1.call-start = ((), (), s32[]{:S(2)}) async-start(), calls=%async_computation.6 | async-start | bytes 1179648 | tf_op jit(solution)/shard_map/all_gather | solution.py:60
  10.6 105.5 %all-gather.7.cloned.1.call-start = ((), (), s32[]{:S(2)}) async-start(), calls=%async_computation.3 | async-start | bytes 4456448 | tf_op jit(solution)/shard_map/all_gather | solution.py:66
  11.4 158.1 %all-gather.9.cloned.1.call-start = ((), (), s32[]{:S(2)}) async-start(), calls=%async_computation.4 | async-start | bytes 4456448 | tf_op jit(solution)/shard_map/all_gather | solution.py:73
  12.0 274.5 %reduce-scatter.9.cloned.1.call-start = ((), (), s32[]{:S(2)}) async-start(), calls=%async_computation.5 | async-start | bytes 1179648 | tf_op jit(solution)/shard_map/reduce_scatter | solution.py:78
  39.6 76.6 %copy-start.2 = (bf16[16,128,128]{2,1,0:T(8,128)(2,1)}, bf16[16,128,128]{2,1,0:T(8,128)(2,1)S(1)}, u32[]{:S(2)}) copy-start(bf16[16,128,128]{2,1,0:T(8,128)(2,1)S(1)} %gather_fusion) | copy-start | bytes 1572868
  46.0 74.5 %copy-start.16 = (bf16[16,128,128]{2,1,0:T(8,128)(2,1)}, bf16[16,128,128]{2,1,0:T(8,128)(2,1)S(1)}, u32[]{:S(2)}) copy-start(bf16[16,128,128]{2,1,0:T(8,128)(2,1)S(1)} %gather_fusion.5) | copy-start | bytes 1572868
  46.6 74.2 %copy-start.14 = (bf16[16,128,128]{2,1,0:T(8,128)(2,1)}, bf16[16,128,128]{2,1,0:T(8,128)(2,1)S(1)}, u32[]{:S(2)}) copy-start(bf16[16,128,128]{2,1,0:T(8,128)(2,1)S(1)} %gather_fusion.6) | copy-start | bytes 1572868
  65.2 145.2 %copy-start.3 = (bf16[16,128,128]{2,1,0:T(8,128)(2,1)}, bf16[16,128,128]{2,1,0:T(8,128)(2,1)S(1)}, u32[]{:S(2)}) copy-start(bf16[16,128,128]{2,1,0:T(8,128)(2,1)S(1)} %gather_fusion.8) | copy-start | bytes 1572868
  75.1 44.3 %copy-start.22 = (bf16[16,128,128]{2,1,0:T(8,128)(2,1)S(1)}, bf16[16,128,128]{2,1,0:T(8,128)(2,1)}, u32[]{:S(2)}) copy-start(bf16[16,128,128]{2,1,0:T(8,128)(2,1)} %gather_fusion.2) | copy-start | bytes 1572868
  116.2 3.2 copy-start
  116.2 3.6 copy-start.20
  117.7 2.4 copy-start.18
  120.1 1.1 copy-start.26
  210.3 3.6 copy-start.12
  210.3 91.8 %reduce-scatter.11.cloned.1.call-start = ((), (), s32[]{:S(2)}) async-start(), calls=%async_computation.7 | async-start | bytes 1179648 | tf_op jit(solution)/shard_map/reduce_scatter | solution.py:89
  210.4 3.5 copy-start.1
  210.4 4.1 copy-start.10
  212.1 2.9 copy-start.8
  213.9 1.7 copy-start.6
  214.5 1.6 copy-start.4
  215.0 1.6 copy-start.24
  215.1 1.6 copy-start.28
  260.1 8.3 %copy-start.21 = (bf16[16,128,128]{2,1,0:T(8,128)(2,1)S(1)}, bf16[16,128,128]{2,1,0:T(8,128)(2,1)}, u32[]{:S(2)}) copy-start(bf16[16,128,128]{2,1,0:T(8,128)(2,1)} %gather_fusion.3) | copy-start | bytes 1572868
  260.1 7.0 %copy-start.23 = (bf16[16,128,128]{2,1,0:T(8,128)(2,1)S(1)}, bf16[16,128,128]{2,1,0:T(8,128)(2,1)}, u32[]{:S(2)}) copy-start(bf16[16,128,128]{2,1,0:T(8,128)(2,1)} %gather_fusion.2) | copy-start | bytes 1572868
  260.1 9.5 %copy-start.19 = (bf16[16,128,128]{2,1,0:T(8,128)(2,1)S(1)}, bf16[16,128,128]{2,1,0:T(8,128)(2,1)}, u32[]{:S(2)}) copy-start(bf16[16,128,128]{2,1,0:T(8,128)(2,1)} %gather_fusion.4) | copy-start | bytes 1572868
  262.5 8.3 %copy-start.17 = (bf16[16,128,128]{2,1,0:T(8,128)(2,1)S(1)}, bf16[16,128,128]{2,1,0:T(8,128)(2,1)}, u32[]{:S(2)}) copy-start(bf16[16,128,128]{2,1,0:T(8,128)(2,1)} %copy-done.16) | copy-start | bytes 1572868
  264.8 7.3 %copy-start.15 = (bf16[16,128,128]{2,1,0:T(8,128)(2,1)S(1)}, bf16[16,128,128]{2,1,0:T(8,128)(2,1)}, u32[]{:S(2)}) copy-start(bf16[16,128,128]{2,1,0:T(8,128)(2,1)} %copy-done.14) | copy-start | bytes 1572868
  269.6 8.4 %copy-start.13 = (bf16[16,128,128]{2,1,0:T(8,128)(2,1)S(1)}, bf16[16,128,128]{2,1,0:T(8,128)(2,1)}, u32[]{:S(2)}) copy-start(bf16[16,128,128]{2,1,0:T(8,128)(2,1)} %gather_fusion.10) | copy-start | bytes 1572868
  270.9 8.4 %copy-start.11 = (bf16[16,128,128]{2,1,0:T(8,128)(2,1)S(1)}, bf16[16,128,128]{2,1,0:T(8,128)(2,1)}, u32[]{:S(2)}) copy-start(bf16[16,128,128]{2,1,0:T(8,128)(2,1)} %gather_fusion.11) | copy-start | bytes 1572868
  272.1 8.3 %copy-start.9 = (bf16[16,128,128]{2,1,0:T(8,128)(2,1)S(1)}, bf16[16,128,128]{2,1,0:T(8,128)(2,1)}, u32[]{:S(2)}) copy-start(bf16[16,128,128]{2,1,0:T(8,128)(2,1)} %gather_fusion.12) | copy-start | bytes 1572868
  273.3 8.3 %copy-start.7 = (bf16[16,128,128]{2,1,0:T(8,128)(2,1)S(1)}, bf16[16,128,128]{2,1,0:T(8,128)(2,1)}, u32[]{:S(2)}) copy-start(bf16[16,128,128]{2,1,0:T(8,128)(2,1)} %gather_fusion.13) | copy-start | bytes 1572868
  273.4 175.9 %all-reduce.5.cloned.1.call-start = ((), (), s32[]{:S(2)}) async-start(), calls=%async_computation.8 | async-start | bytes 16777216
  275.8 7.1 %copy-start.5 = (bf16[16,128,128]{2,1,0:T(8,128)(2,1)S(1)}, bf16[16,128,128]{2,1,0:T(8,128)(2,1)}, u32[]{:S(2)}) copy-start(bf16[16,128,128]{2,1,0:T(8,128)(2,1)} %gather_fusion.14) | copy-start | bytes 1572868
  278.0 6.0 %copy-start.25 = (bf16[16,128,128]{2,1,0:T(8,128)(2,1)S(1)}, bf16[16,128,128]{2,1,0:T(8,128)(2,1)}, u32[]{:S(2)}) copy-start(bf16[16,128,128]{2,1,0:T(8,128)(2,1)} %gather_fusion.15) | copy-start | bytes 1572868
  285.2 0.7 copy-start.27
Sparse Core Ops, SparseCore 0:
  10.3 26.9 all-gather.4
  39.6 23.2 all-gather.10
  65.0 51.1 all-gather.6
  118.2 51.2 all-gather.8
  210.5 28.6 reduce-scatter.8
  273.5 28.6 reduce-scatter.10
  305.9 143.2 all-reduce.4
where the time goes:
time: 463 us; the launch traced here: 461 us
  waiting for transfers between devices  284 us (61%)
  matrix products  76.9 us (17%)
  other arithmetic  52.9 us (11%)
  local copies, waits for them, and re-layouts  31.5 us (7%)
  between operations  14.8 us (3%)
    unnamed x8, waiting for transfers between devices  147 us
    all_gather x1, waiting for transfers between devices, per_device(): lax.all_gather(down_weight, 'row', axis=0, tiled=True)  46.6 us
    all_gather x1, waiting for transfers between devices, per_device(): lax.all_gather(up_weight, 'row', axis=0, tiled=True)  41.1 us
    all_gather x1, waiting for transfers between devices, per_device(): lax.all_gather(tokens, 'col', axis=1, tiled=True)  21.2 us
    scatter-add x8, other arithmetic, up_transpose(): summed = summed.at[:, row_ids[:, slot_index], :].add(product)  21 us
    scatter-add x8, other arithmetic, down_apply(): out_part = out_part.at[:, col_ids[:, slot_index], :].add(product)  21 us
    dot_general x8, matrix products, up_transpose(): jnp.einsum('tjb,jab->tja', grad_piece, panel_blocks[:, slot_index], prefe...  19.9 us
    dot_general x8, matrix products, down_apply(): jnp.einsum('tia,iab->tib', hidden_piece, weight_slot, preferred_element_t...  18.4 us
  transfers between devices with their start and end apart: 7, of which 6 were waited for; matrix products, arithmetic and copies ran while one was open for 25% of the time, Pallas kernels for 0%

commit v1 on v0

--- a/solution.py
+++ b/solution.py
@@ -56,7 +56,12 @@
     block_size = up_weight.shape[2]
     slot_count = up_weight.shape[1]
     token_whole, grad_whole = (
-        lax.all_gather(tokens, "col", axis=1, tiled=True),
+        jnp.concatenate(
+            lax.all_to_all(
+                jnp.stack([tokens for _ in range(lax.axis_size("col"))], axis=0), "col", 0, 0
+            ),
+            axis=1,
+        ),
         lax.all_gather(grad_out, "col", axis=1, tiled=True),
     )
     block_count = token_whole.shape[1] // block_size

time: 463 us -> 440 us (0.950)
  waiting for transfers between devices: 284 us -> 258 us
  starting transfers between devices: 0.28 us -> 6.17 us
    all_gather x1 -> x0, waiting for transfers between devices: 21.2 us -> none  [per_device(): lax.all_gather(tokens, 'col', axis=1, tiled=True)]
    all_to_all x0 -> x1, waiting for transfers between devices: none -> 18.8 us  [per_device(): lax.all_to_all(jnp.stack([tokens for _ in range(lax.axis_size('col'))], a...]
    all_gather x1, waiting for transfers between devices: 14.8 us -> 0.01 us  [per_device(): lax.all_gather(grad_out, 'col', axis=1, tiled=True)]
    all_gather x1, waiting for transfers between devices: 41.1 us -> 32 us  [per_device(): lax.all_gather(up_weight, 'row', axis=0, tiled=True)]
    all_to_all x0 -> x1, starting transfers between devices: none -> 5.97 us  [per_device(): lax.all_to_all(jnp.stack([tokens for _ in range(lax.axis_size('col'))], a...]
    unnamed x8 -> x7, waiting for transfers between devices: 147 us -> 147 us
  transfers between devices with their start and end apart: 7 -> 7, of which waited for: 6 -> 5; matrix products, arithmetic and copies ran while one was open for 25% -> 25% of each run, Pallas kernels for 0% -> 0%
where the time goes in v1:
time: 440 us; the launch traced here: 438 us
  waiting for transfers between devices  258 us (59%)
  matrix products  76.9 us (17%)
  other arithmetic  49 us (11%)
  local copies, waits for them, and re-layouts  32.6 us (7%)
  between operations  14.8 us (3%)
  starting transfers between devices  6.17 us (1%)
    unnamed x7, waiting for transfers between devices  147 us
    all_gather x1, waiting for transfers between devices, per_device(): lax.all_gather(down_weight, 'row', axis=0, tiled=True)  46.9 us
    all_gather x1, waiting for transfers between devices, per_device(): lax.all_gather(up_weight, 'row', axis=0, tiled=True)  32 us
    scatter-add x8, other arithmetic, up_transpose(): summed = summed.at[:, row_ids[:, slot_index], :].add(product)  21 us
    scatter-add x8, other arithmetic, down_apply(): out_part = out_part.at[:, col_ids[:, slot_index], :].add(product)  21 us
    dot_general x8, matrix products, up_transpose(): jnp.einsum('tjb,jab->tja', grad_piece, panel_blocks[:, slot_index], prefe...  20.1 us
    all_to_all x1, waiting for transfers between devices, per_device(): lax.all_to_all(jnp.stack([tokens for _ in range(lax.axis_size('col'))], a...  18.8 us
    dot_general x8, matrix products, down_apply(): jnp.einsum('tia,iab->tib', hidden_piece, weight_slot, preferred_element_t...  18.4 us
  transfers between devices with their start and end apart: 7, of which 5 were waited for; matrix products, arithmetic and copies ran while one was open for 25% of the time, Pallas kernels for 0%

profile of v1, /device:TPU:1, one launch (start us, length us, event | category | flops | bytes accessed | tf_op | source)
XLA Modules:
  0.0 437.6 jit_solution(13048675917672454199)
XLA Ops:
  7.2 1.7 copy.117
  12.6 6.0 %all-to-all-start = ((bf16[8,128,512]{1,2,0:T(8,128)(2,1)}), bf16[8,128,512]{1,2,0:T(8,128)(2,1)S(1)}, u32[]{:S(2)}, u32[]{:S(2)}) async-start(bf16[8,128,512]{1,2,0:T(8,128)(2,1)} %stack.83), calls=%async_computation | async-start | bytes 2097152 | tf_op jit(solution)/shard_map/all_to_all | solution.py:60
  18.7 18.8 %all-to-all-done = bf16[8,128,512]{1,2,0:T(8,128)(2,1)S(1)} async-done(((bf16[8,128,512]{1,2,0:T(8,128)(2,1)}), bf16[8,128,512]{1,2,0:T(8,128)(2,1)S(1)}, u32[]{:S(2)}, u32[]{:S(2)}) %all-to-all-start) | async-done | bytes 1048608 | tf_op jit(solution)/shard_map/all_to_all | solution.py:60
  38.9 1.5 gather_fusion.1
  40.3 1.4 gather_fusion.2
  41.8 1.4 gather_fusion.3
  43.2 1.4 gather_fusion.4
  44.6 1.4 gather_fusion.5
  46.0 1.4 gather_fusion.6
  47.4 1.4 gather_fusion.7
  48.9 1.6 copy.118
  52.6 1.4 gather_fusion.10
  54.0 1.4 gather_fusion.11
  55.4 1.4 gather_fusion.12
  56.8 1.4 gather_fusion.13
  59.6 1.4 gather_fusion.15
  61.0 32.0 %all-gather.4.cloned.1.call-done = bf16[16,8,128,128]{3,2,0,1:T(8,128)(2,1)} async-done(((bf16[1,8,128,128]{3,2,0,1:T(8,128)(2,1)}), bf16[16,8,128,128]{3,2,0,1:T(8,128)(2,1)}) %all-gather.4.cloned.1.call-update) | async-done | bytes 4194320 | tf_op jit(solution)/shard_map/all_gather | solution.py:71
  93.0 1.5 fusion.73
  94.6 1.5 convolution_add_fusion.13
  98.0 1.6 multiply_convert_fusion
  99.6 46.9 %all-gather.6.cloned.1.call-done = bf16[16,8,128,128]{3,2,0,1:T(8,128)(2,1)} async-done(((bf16[1,8,128,128]{3,2,0,1:T(8,128)(2,1)}), bf16[16,8,128,128]{3,2,0,1:T(8,128)(2,1)}) %all-gather.6.cloned.1.call-update) | async-done | bytes 4194320 | tf_op jit(solution)/shard_map/all_gather | solution.py:78
  146.5 2.3 fusion.83
  149.0 2.6 scatter_fusion
  151.6 2.3 fusion.84
  153.9 2.6 scatter_fusion.1
  156.5 2.3 fusion.85
  158.8 2.6 scatter_fusion.2
  161.4 2.3 fusion.86
  163.7 2.6 scatter_fusion.3
  166.3 2.3 fusion.87
  168.6 2.6 scatter_fusion.4
  171.2 2.3 fusion.88
  173.5 2.6 scatter_fusion.5
  176.2 2.3 fusion.89
  178.4 2.8 scatter_fusion.6
  181.2 2.3 fusion.90
  183.5 2.6 scatter_fusion.7
  187.4 1.7 fusion.56
  189.1 1.8 convolution_add_fusion.6
  194.7 2.5 fusion.75
  197.4 2.6 scatter_fusion.8
  200.0 2.5 fusion.76
  202.5 2.6 scatter_fusion.9
  205.1 2.5 fusion.77
  207.6 2.6 scatter_fusion.10
  210.3 2.5 fusion.78
  212.8 2.6 scatter_fusion.11
  215.4 2.5 fusion.79
  217.9 2.6 scatter_fusion.12
  220.5 2.5 fusion.80
  223.0 2.6 scatter_fusion.13
  225.6 2.5 fusion.81
  228.1 2.6 scatter_fusion.14
  230.8 2.5 fusion.82
  233.3 2.8 scatter_fusion.15
  237.2 2.4 fusion.3
  239.7 2.3 fusion.19
  242.0 2.3 fusion.5
  250.5 2.3 fusion.17
  252.9 2.3 fusion.21
  265.4 13.8 %reduce-scatter.11.cloned.1.call-done = bf16[128,4,128]{2,0,1:T(8,128)(2,1)} async-done(((bf16[128,32,128]{2,0,1:T(8,128)(2,1)}), bf16[128,4,128]{2,0,1:T(8,128)(2,1)}) %reduce-scatter.11.cloned.1.call-update) | async-done | bytes 131088 | tf_op jit(solution)/shard_map/reduce_scatter | solution.py:94
  281.1 145.2 %all-reduce.5.cloned.1.call-done = (bf16[16,8,128,128]{3,2,0,1:T(8,128)(2,1)}, bf16[16,8,128,128]{3,2,0,1:T(8,128)(2,1)}) async-done(((bf16[16,8,128,128]{3,2,0,1:T(8,128)(2,1)}, bf16[16,8,128,128]{3,2,0,1:T(8,128)(2,1)}), (bf16[16,8,128,128]{3,2,0,1:T(8,128)(2,1)}, bf16[16,8,128,128]{3,2,0,1:T(8,128)(2,1)})) %all-reduce.5.cloned.1.call-update) | async-done | bytes 8388624
  426.2 2.3 fusion.91
  428.5 2.3 fusion.92
  (128 shorter events, 35.0 us)
Async XLA Ops:
  7.2 11.4 %copy-start.29 = (s32[16,8]{0,1:T(8,128)S(1)}, s32[16,8]{0,1:T(8,128)}, u32[]{:S(2)}) copy-start(s32[16,8]{0,1:T(8,128)} %param.10) | copy-start | bytes 1540
  7.2 11.4 %copy-start.28 = (s32[16,8]{0,1:T(8,128)S(1)}, s32[16,8]{0,1:T(8,128)}, u32[]{:S(2)}) copy-start(s32[16,8]{0,1:T(8,128)} %param.12) | copy-start | bytes 1540
  7.2 41.7 %all-gather.8.cloned.1.call-start = ((), (), s32[]{:S(2)}) async-start(), calls=%async_computation.6 | async-start | bytes 1179648 | tf_op jit(solution)/shard_map/all_gather | solution.py:65
  8.9 84.1 %all-gather.4.cloned.1.call-start = ((), (), s32[]{:S(2)}) async-start(), calls=%async_computation.3 | async-start | bytes 4456448 | tf_op jit(solution)/shard_map/all_gather | solution.py:71
  9.7 136.8 %all-gather.6.cloned.1.call-start = ((), (), s32[]{:S(2)}) async-start(), calls=%async_computation.4 | async-start | bytes 4456448 | tf_op jit(solution)/shard_map/all_gather | solution.py:78
  12.6 25.0 %all-to-all-start = ((bf16[8,128,512]{1,2,0:T(8,128)(2,1)}), bf16[8,128,512]{1,2,0:T(8,128)(2,1)S(1)}, u32[]{:S(2)}, u32[]{:S(2)}) async-start(bf16[8,128,512]{1,2,0:T(8,128)(2,1)} %stack.83), calls=%async_computation | async-start | bytes 2097152 | tf_op jit(solution)/shard_map/all_to_all | solution.py:60
  18.5 245.1 %reduce-scatter.9.cloned.1.call-start = ((), (), s32[]{:S(2)}) async-start(), calls=%async_computation.5 | async-start | bytes 1179648 | tf_op jit(solution)/shard_map/reduce_scatter | solution.py:83
  38.9 54.1 %copy-start.2 = (bf16[16,128,128]{2,1,0:T(8,128)(2,1)}, bf16[16,128,128]{2,1,0:T(8,128)(2,1)S(1)}, u32[]{:S(2)}) copy-start(bf16[16,128,128]{2,1,0:T(8,128)(2,1)S(1)} %gather_fusion) | copy-start | bytes 1572868
  51.1 136.2 %copy-start.3 = (bf16[16,128,128]{2,1,0:T(8,128)(2,1)}, bf16[16,128,128]{2,1,0:T(8,128)(2,1)S(1)}, u32[]{:S(2)}) copy-start(bf16[16,128,128]{2,1,0:T(8,128)(2,1)S(1)} %gather_fusion.8) | copy-start | bytes 1572868
  52.6 42.0 %copy-start.24 = (bf16[16,128,128]{2,1,0:T(8,128)(2,1)S(1)}, bf16[16,128,128]{2,1,0:T(8,128)(2,1)}, u32[]{:S(2)}) copy-start(bf16[16,128,128]{2,1,0:T(8,128)(2,1)} %gather_fusion.1) | copy-start | bytes 1572868
  56.8 39.3 %copy-start.22 = (bf16[16,128,128]{2,1,0:T(8,128)(2,1)S(1)}, bf16[16,128,128]{2,1,0:T(8,128)(2,1)}, u32[]{:S(2)}) copy-start(bf16[16,128,128]{2,1,0:T(8,128)(2,1)} %gather_fusion.2) | copy-start | bytes 1572868
  93.0 3.1 copy-start
  93.0 3.4 copy-start.20
  94.6 2.2 copy-start.18
  96.1 1.1 copy-start.16
  96.5 1.1 copy-start.14
  96.8 1.1 copy-start.27
  187.3 3.6 copy-start.12
  187.3 92.0 %reduce-scatter.11.cloned.1.call-start = ((), (), s32[]{:S(2)}) async-start(), calls=%async_computation.7 | async-start | bytes 1179648 | tf_op jit(solution)/shard_map/reduce_scatter | solution.py:94
  187.3 3.5 copy-start.1
  187.4 4.1 copy-start.10
  189.1 2.9 copy-start.8
  190.9 1.7 copy-start.6
  191.5 1.6 copy-start.4
  192.0 1.6 copy-start.25
  192.0 1.6 copy-start.31
  237.2 8.3 %copy-start.21 = (bf16[16,128,128]{2,1,0:T(8,128)(2,1)S(1)}, bf16[16,128,128]{2,1,0:T(8,128)(2,1)}, u32[]{:S(2)}) copy-start(bf16[16,128,128]{2,1,0:T(8,128)(2,1)} %gather_fusion.3) | copy-start | bytes 1572868
  237.2 7.1 %copy-start.23 = (bf16[16,128,128]{2,1,0:T(8,128)(2,1)S(1)}, bf16[16,128,128]{2,1,0:T(8,128)(2,1)}, u32[]{:S(2)}) copy-start(bf16[16,128,128]{2,1,0:T(8,128)(2,1)} %gather_fusion.2) | copy-start | bytes 1572868
  237.2 9.5 %copy-start.19 = (bf16[16,128,128]{2,1,0:T(8,128)(2,1)S(1)}, bf16[16,128,128]{2,1,0:T(8,128)(2,1)}, u32[]{:S(2)}) copy-start(bf16[16,128,128]{2,1,0:T(8,128)(2,1)} %gather_fusion.4) | copy-start | bytes 1572868
  239.7 8.3 %copy-start.17 = (bf16[16,128,128]{2,1,0:T(8,128)(2,1)S(1)}, bf16[16,128,128]{2,1,0:T(8,128)(2,1)}, u32[]{:S(2)}) copy-start(bf16[16,128,128]{2,1,0:T(8,128)(2,1)} %gather_fusion.5) | copy-start | bytes 1572868
  242.0 7.3 %copy-start.15 = (bf16[16,128,128]{2,1,0:T(8,128)(2,1)S(1)}, bf16[16,128,128]{2,1,0:T(8,128)(2,1)}, u32[]{:S(2)}) copy-start(bf16[16,128,128]{2,1,0:T(8,128)(2,1)} %gather_fusion.6) | copy-start | bytes 1572868
  246.8 8.4 %copy-start.13 = (bf16[16,128,128]{2,1,0:T(8,128)(2,1)S(1)}, bf16[16,128,128]{2,1,0:T(8,128)(2,1)}, u32[]{:S(2)}) copy-start(bf16[16,128,128]{2,1,0:T(8,128)(2,1)} %gather_fusion.10) | copy-start | bytes 1572868
  248.0 8.4 %copy-start.11 = (bf16[16,128,128]{2,1,0:T(8,128)(2,1)S(1)}, bf16[16,128,128]{2,1,0:T(8,128)(2,1)}, u32[]{:S(2)}) copy-start(bf16[16,128,128]{2,1,0:T(8,128)(2,1)} %gather_fusion.11) | copy-start | bytes 1572868
  249.2 8.3 %copy-start.9 = (bf16[16,128,128]{2,1,0:T(8,128)(2,1)S(1)}, bf16[16,128,128]{2,1,0:T(8,128)(2,1)}, u32[]{:S(2)}) copy-start(bf16[16,128,128]{2,1,0:T(8,128)(2,1)} %gather_fusion.12) | copy-start | bytes 1572868
  250.5 8.3 %copy-start.7 = (bf16[16,128,128]{2,1,0:T(8,128)(2,1)S(1)}, bf16[16,128,128]{2,1,0:T(8,128)(2,1)}, u32[]{:S(2)}) copy-start(bf16[16,128,128]{2,1,0:T(8,128)(2,1)} %gather_fusion.13) | copy-start | bytes 1572868
  250.5 175.7 %all-reduce.5.cloned.1.call-start = ((), (), s32[]{:S(2)}) async-start(), calls=%async_computation.8 | async-start | bytes 16777216
  252.9 7.1 %copy-start.5 = (bf16[16,128,128]{2,1,0:T(8,128)(2,1)S(1)}, bf16[16,128,128]{2,1,0:T(8,128)(2,1)}, u32[]{:S(2)}) copy-start(bf16[16,128,128]{2,1,0:T(8,128)(2,1)} %gather_fusion.14) | copy-start | bytes 1572868
  255.2 6.0 %copy-start.26 = (bf16[16,128,128]{2,1,0:T(8,128)(2,1)S(1)}, bf16[16,128,128]{2,1,0:T(8,128)(2,1)}, u32[]{:S(2)}) copy-start(bf16[16,128,128]{2,1,0:T(8,128)(2,1)} %gather_fusion.15) | copy-start | bytes 1572868
  262.4 0.7 copy-start.30
Sparse Core Ops, SparseCore 0:
  10.3 29.0 all-gather.7
  41.6 51.3 all-gather.3
  95.2 51.2 all-gather.5
  187.4 28.6 reduce-scatter.8
  250.6 28.6 reduce-scatter.10
  282.9 143.2 all-reduce.4
